TPU v7x, 32 devices: a whole 2x2x4 slice. The times are simulated.
32 devices in a mesh: groups: 2 (over y), batch: 16 (over z, x, core).
Axes of the slice: x: 2, y: 2, z: 4, core: 2. Of those that a mesh axis runs over, the one named last changes fastest.
Arguments:
- queries: bfloat16 [64, 34, 8192], P(('groups', 'batch')), parts along dimension 0, may hold values from -6 to 6
- key_vectors: bfloat16 [64, 34, 8192], P(('groups', 'batch')), parts along dimension 0, may hold values from -0.5 to 0.5
- values: bfloat16 [64, 34, 8192], P(('groups', 'batch')), parts along dimension 0, may hold values from -6 to 6
- gate_logits: bfloat16 [64, 34, 8192], P(('groups', 'batch')), parts along dimension 0, may hold values from -6 to 6
- decay_rates: float32 [64], replicated, may hold values from 0.003 to 0.08
- norm_gain: float32 [8192], replicated, may hold values from 0.1 to 1.9
- pool_states: bfloat16 [32, 8192, 128], P(('groups', 'batch')), parts along dimension 0, may hold values from -1.75 to 1.75
- pool_entry: int32 [64], P(('groups', 'batch')), parts along dimension 0, may hold values from 0 to 15
Outputs:
- mixed: bfloat16 [64, 34, 8192], P(('groups', 'batch')), parts along dimension 0
- new_states: bfloat16 [64, 8192, 128], P('groups', 'batch'), parts along dimension 0
There are 2 independent parts, one for each index of `groups`. A program takes and returns all parts, laid end to end along the dimension named above; an argument that names none is the same for every part. Nothing has to cross between parts.
Inputs may be any that keep to these rules, and one draw needn't show every extreme that they name: `pool_entry`: entry e is the only entry of the pool shard on batch device e; several requests may name the same entry.
All inputs are finite; a program needn't handle non-finite values.
Results may differ from a plain program's by a relative error of at most 0.001.
Values may be sent and summed in bfloat16 or wider, within the bound.
No kernel may reach another device: no remote copies, remote signals or barrier semaphores. Data moves between devices by JAX's collectives and lax.ppermute only.
A program may use at most 64 MiB of HBM per device.

v0:
```python
import jax
import jax.numpy as jnp
from jax import lax
from jax.sharding import PartitionSpec as P


def finish_output(attended, gate_logits, norm_gain):
    mean_square = jnp.mean(attended * attended, axis=-1, keepdims=True)
    scaled = attended * lax.rsqrt(mean_square + 1e-05) * norm_gain
    return (scaled * jax.nn.sigmoid(gate_logits.astype(jnp.float32))).astype(jnp.bfloat16)


def attend(query_part, key_part, value_part, resumed, rates_here):
    length = query_part.shape[1]
    highest = lax.Precision.HIGHEST
    positions = jnp.arange(1, length + 1).astype(jnp.float32)
    decay_now = jnp.exp(-positions[:, None] * rates_here[None, :])
    from_state = jnp.einsum(
        "rtgd,rgde->rtge", query_part, resumed, preferred_element_type=jnp.float32
    )
    from_state = from_state * decay_now[None, :, :, None]
    key_wide = key_part.astype(jnp.float32)
    value_wide = value_part.astype(jnp.float32)
    distance = positions[:, None] - positions[None, :]
    decay_pair = jnp.where(
        (distance >= 0.0)[:, :, None],
        jnp.exp(-jnp.maximum(distance, 0.0)[:, :, None] * rates_here),
        0.0,
    )
    scores = (
        jnp.einsum("rtgd,rsgd->rtsg", query_part, key_part, preferred_element_type=jnp.float32)
        * decay_pair[None]
    )
    in_block = jnp.einsum("rtsg,rsge->rtge", scores, value_wide, precision=highest)
    tail_decay = jnp.exp(-(float(length) - positions)[:, None] * rates_here[None, :])
    weighted_keys = key_wide * tail_decay[None, :, :, None]
    updated = jnp.exp(-float(length) * rates_here)[None, :, None, None] * resumed.astype(
        jnp.float32
    )
    updated = updated + jnp.einsum("rsgd,rsge->rgde", weighted_keys, value_wide, precision=highest)
    return (from_state + in_block, updated)


def on_device(
    queries, key_vectors, values, gate_logits, decay_rates, norm_gain, pool_states, pool_entry
):
    req_dev, length, feature_width = queries.shape
    head_count = decay_rates.shape[0]
    head_size = pool_states.shape[2]
    entries = lax.all_gather(pool_entry, "batch", axis=0, tiled=True)
    spread = lax.all_to_all(pool_states, "batch", split_axis=1, concat_axis=0, tiled=True)
    chosen = jnp.take(spread, entries, axis=0)
    resumed = lax.all_to_all(chosen, "batch", split_axis=0, concat_axis=1, tiled=True)
    resumed = resumed.reshape(req_dev, head_count, head_size, head_size)
    shaped = (req_dev, length, head_count, head_size)
    attended, updated = attend(
        queries.reshape(shaped),
        key_vectors.reshape(shaped),
        values.reshape(shaped),
        resumed,
        decay_rates,
    )
    attended = attended.reshape(req_dev, length, feature_width)
    local_states = updated.astype(jnp.bfloat16).reshape(req_dev, feature_width, head_size)
    new_states = lax.all_to_all(local_states, "batch", split_axis=1, concat_axis=0, tiled=True)
    mixed = finish_output(attended, gate_logits, norm_gain)
    return (mixed, new_states)


def solution(mesh):
    placed = (
        P(("groups", "batch"), None, None),
        P(("groups", "batch"), None, None),
        P(("groups", "batch"), None, None),
        P(("groups", "batch"), None, None),
        P(),
        P(),
        P(("groups", "batch"), None, None),
        P(("groups", "batch")),
    )
    return jax.shard_map(
        on_device,
        mesh=mesh,
        in_specs=placed,
        out_specs=(P(("groups", "batch"), None, None), P("groups", "batch", None)),
        check_vma=False,
    )
```

profile of v0, /device:TPU:11, one launch (start us, length us, event | category | flops | bytes accessed | tf_op | source)
XLA Modules:
  0.0 375.3 jit_solution(9554630048918124368)
XLA Ops:
  0.6 7.5 %copy.67 = bf16[1,8192,128]{2,0,1:T(2,128)(2,1)} copy(bf16[1,8192,128]{2,1,0:T(8,128)(2,1)} %param.14) | data formatting | bytes 4194304 | tf_op args[6]
  8.1 0.5 broadcast.157
  8.6 45.2 %reduce.1 = bf16[8192,128]{1,0:T(8,128)(2,1)S(1)} reduce(bf16[8192,1,128]{2,1,0:T(2,128)(2,1)} %bitcast.38, bf16[]{:T(256)} %broadcast.157), dimensions={1}, to_apply=%bitcast.34.reduce_sub_computation | reduce | bytes 4194306
  53.8 2.0 reshape.201
  55.8 0.0 copy-start.7
  55.8 0.0 copy-start.6
  55.8 6.7 %all-to-all-start = ((bf16[16,2,32768]{2,1,0:T(2,128)(2,1)}), bf16[16,2,32768]{2,1,0:T(2,128)(2,1)S(1)}, u32[]{:S(2)}, u32[]{:S(2)}) async-start(bf16[16,2,32768]{2,1,0:T(2,128)(2,1)} %reshape.201), calls=%async_computation | async-start | bytes 4194304 | tf_op jit(solution)/shard_map/all_to_all | solution.py:51
  62.5 0.0 copy-done.7
  62.5 0.6 dynamic-slice
  63.7 0.0 copy-done.6
  63.7 0.2 dynamic-update-slice
  64.0 43.8 %all-reduce = s32[32]{0:T(128)S(1)} all-reduce(s32[32]{0:T(128)S(1)} %dynamic-update-slice), channel_id=1, replica_groups=mesh['groups'=2,'batch'=16] {'batch'}, use_global_device_ids=true, to_apply=%add | all-reduce | flops 32 | bytes 256
  107.8 2.2 all-to-all-done
  110.0 6.7 %reshape.202 = bf16[8192,1,128]{2,1,0:T(2,128)(2,1)} reshape(bf16[16,2,32768]{2,1,0:T(2,128)(2,1)S(1)} %all-to-all-done) | data formatting | bytes 4194304
  116.7 2.5 copy.49
  119.2 3.1 gather_fusion
  122.3 4.7 %broadcast_select_fusion = bf16[32,512,128]{2,1,0:T(8,128)(2,1)} fusion(bf16[32,512,128]{2,1,0:T(8,128)(2,1)} %gather_fusion, pred[32]{0:T(512)(128)(4,1)S(1)} %compare_and_fusion), kind=kLoop, calls=%fused_computation.2 | loop fusion | flops 2097152 | bytes 8388640 | tf_op jit(solution)/shard_map/jit(_take)/select_n | solution.py:52
  126.9 0.0 copy-start.2
  126.9 6.2 %all-to-all-start.1 = ((bf16[32,512,128]{2,1,0:T(8,128)(2,1)}), bf16[32,512,128]{2,1,0:T(8,128)(2,1)}, u32[]{:S(2)}, u32[]{:S(2)}) async-start(bf16[32,512,128]{2,1,0:T(8,128)(2,1)} %broadcast_select_fusion), calls=%async_computation.1 | async-start | bytes 8388608 | tf_op jit(solution)/shard_map/all_to_all | solution.py:53
  133.2 0.0 copy-done.2
  133.2 0.0 copy-start.5
  133.2 0.9 reshape.183
  134.1 3.2 reshape.184
  137.3 0.0 copy-done.5
  137.3 0.1 multiply_exponential_fusion
  137.4 88.3 %all-to-all-done.1 = bf16[32,512,128]{2,1,0:T(8,128)(2,1)} async-done(((bf16[32,512,128]{2,1,0:T(8,128)(2,1)}), bf16[32,512,128]{2,1,0:T(8,128)(2,1)}, u32[]{:S(2)}, u32[]{:S(2)}) %all-to-all-start.1) | async-done | bytes 4194336 | tf_op jit(solution)/shard_map/all_to_all | solution.py:53
  225.7 2.6 copy.36
  228.3 0.0 copy-start
  228.3 9.0 %add_convert_fusion = bf16[2,64,128,128]{3,2,1,0:T(8,128)(2,1)S(1)} fusion(bf16[2,64,128,128]{3,2,1,0:T(8,128)(2,1)S(1)} %bitcast.35, f32[64]{0:T(128)S(1)} %multiply_exponential_fusion.2, f32[34,64]{0,1:T(8,128)S(1)} %get-tuple-element.2, bf16[2,34,64,128]{3,2,0,1:T(8,128)(2,1)S(1)} %reshape.184, bf16[2,34,64,128]{3,2,0,1:T(8,128)(2,1)S(1)} %reshape.183), kind=kOutput, calls=%fused_computation.1 | convolution fusion | flops 865140736 | bytes 10625792 | tf_op jit(solution)/shard_map/rsgd,rsge->rgde/dot_general | solution.py:40
  237.3 0.0 copy-done
  237.3 35.5 %copy.46 = bf16[2,8192,128]{2,0,1:T(2,128)(2,1)} copy(bf16[2,8192,128]{2,1,0:T(8,128)(2,1)S(1)} %bitcast.40) | data formatting | bytes 8388608 | tf_op jit(solution)/shard_map/reshape | solution.py:64
  272.8 4.8 %all-to-all-start.2 = ((bf16[2,8192,128]{2,0,1:T(2,128)(2,1)}), bf16[2,8192,128]{2,0,1:T(2,128)(2,1)}, u32[]{:S(2)}, u32[]{:S(2)}) async-start(bf16[2,8192,128]{2,0,1:T(2,128)(2,1)} %copy.46), calls=%async_computation.2 | async-start | bytes 8388608 | tf_op jit(solution)/shard_map/all_to_all | solution.py:65
  277.6 3.2 reshape.182
  280.8 0.1 subtract_compare_fusion
  280.8 0.1 fusion.13
  280.9 0.2 exponential_select_fusion
  281.2 1.6 fusion.9
  282.7 0.0 copy-start.1
  282.7 3.1 fusion
  285.9 0.0 copy-done.1
  285.9 1.8 multiply_reduce_fusion
  287.6 1.8 copy.42
  289.4 0.0 copy-start.3
  289.4 0.0 copy-start.4
  289.4 2.9 reshape.185
  292.4 0.1 copy.43
  292.5 0.0 copy-done.3
  292.5 0.0 copy-done.4
  292.5 3.5 fusion.3
  296.0 74.1 %all-to-all-done.2 = bf16[2,8192,128]{2,0,1:T(2,128)(2,1)} async-done(((bf16[2,8192,128]{2,0,1:T(2,128)(2,1)}), bf16[2,8192,128]{2,0,1:T(2,128)(2,1)}, u32[]{:S(2)}, u32[]{:S(2)}) %all-to-all-start.2) | async-done | bytes 4194336 | tf_op jit(solution)/shard_map/all_to_all | solution.py:65
  370.1 5.2 %copy.47 = bf16[16,2,512,128]{3,2,1,0:T(8,128)(2,1)} copy(bf16[16,2,512,128]{3,1,2,0:T(2,128)(2,1)} %bitcast.9) | data formatting | bytes 8388608 | tf_op jit(solution)/shard_map/all_to_all | solution.py:65
  (8 shorter events, 0.0 us)
Async XLA Ops:
  55.8 6.7 %copy-start.7 = (u32[32]{0:T(128)S(1)}, u32[32]{0:T(128)}, u32[]{:S(2)}) copy-start(u32[32]{0:T(128)} %constant.40) | copy-start | bytes 388
  55.8 7.9 %copy-start.6 = (s32[2]{0:T(128)S(1)}, s32[2]{0:T(128)}, u32[]{:S(2)}) copy-start(s32[2]{0:T(128)} %param.15) | copy-start | bytes 28
  55.8 54.2 %all-to-all-start = ((bf16[16,2,32768]{2,1,0:T(2,128)(2,1)}), bf16[16,2,32768]{2,1,0:T(2,128)(2,1)S(1)}, u32[]{:S(2)}, u32[]{:S(2)}) async-start(bf16[16,2,32768]{2,1,0:T(2,128)(2,1)} %reshape.201), calls=%async_computation | async-start | bytes 4194304 | tf_op jit(solution)/shard_map/all_to_all | solution.py:51
  126.9 6.3 %copy-start.2 = (bf16[2,34,8192]{2,0,1:T(2,128)(2,1)S(1)}, bf16[2,34,8192]{2,0,1:T(2,128)(2,1)}, u32[]{:S(2)}) copy-start(bf16[2,34,8192]{2,0,1:T(2,128)(2,1)} %param.9) | copy-start | bytes 3342340
  126.9 98.7 %all-to-all-start.1 = ((bf16[32,512,128]{2,1,0:T(8,128)(2,1)}), bf16[32,512,128]{2,1,0:T(8,128)(2,1)}, u32[]{:S(2)}, u32[]{:S(2)}) async-start(bf16[32,512,128]{2,1,0:T(8,128)(2,1)} %broadcast_select_fusion), calls=%async_computation.1 | async-start | bytes 8388608 | tf_op jit(solution)/shard_map/all_to_all | solution.py:53
  133.2 4.1 %copy-start.5 = (f32[64]{0:T(128)S(1)}, f32[64]{0:T(128)}, u32[]{:S(2)}) copy-start(f32[64]{0:T(128)} %param.12) | copy-start | bytes 772
  228.3 9.0 %copy-start = (bf16[2,16,512,128]{3,2,1,0:T(8,128)(2,1)}, bf16[2,16,512,128]{3,2,1,0:T(8,128)(2,1)S(1)}, u32[]{:S(2)}) copy-start(bf16[2,16,512,128]{3,2,1,0:T(8,128)(2,1)S(1)} %copy.36) | copy-start | bytes 12582916
  272.8 97.2 %all-to-all-start.2 = ((bf16[2,8192,128]{2,0,1:T(2,128)(2,1)}), bf16[2,8192,128]{2,0,1:T(2,128)(2,1)}, u32[]{:S(2)}, u32[]{:S(2)}) async-start(bf16[2,8192,128]{2,0,1:T(2,128)(2,1)} %copy.46), calls=%async_computation.2 | async-start | bytes 8388608 | tf_op jit(solution)/shard_map/all_to_all | solution.py:65
  282.7 3.1 copy-start.1
  289.4 3.1 copy-start.3
  289.4 3.1 copy-start.4
where the time goes:
time: 376 us; the launch traced here: 375 us
  waiting for transfers between devices  165 us (44%)
  local copies, waits for them, and re-layouts  78.4 us (21%)
  other arithmetic  53.9 us (14%)
  blocking collectives  43.8 us (12%)
  starting transfers between devices  17.7 us (5%)
  matrix products  15.4 us (4%)
    all_to_all x1, waiting for transfers between devices, on_device(): lax.all_to_all(chosen, 'batch', split_axis=0, concat_axis=1, tiled=True)  88.3 us
    all_to_all x1, waiting for transfers between devices, on_device(): lax.all_to_all(local_states, 'batch', split_axis=1, concat_axis=0, tiled=...  74.1 us
    unnamed x1, other arithmetic  45.2 us
    unnamed x1, blocking collectives  43.8 us
    reshape x1, local copies, waits for them, and re-layouts, on_device(): updated.astype(jnp.bfloat16).reshape(req_dev, feature_width, head_size)  35.5 us
    unnamed x24, local copies, waits for them, and re-layouts  20 us
    dot_general x1, matrix products, attend(): jnp.einsum('rsgd,rsge->rgde', weighted_keys, value_wide, precision=highest)  8.99 us
  transfers between devices with their start and end apart: 3, of which 3 were waited for; matrix products, arithmetic and copies ran while one was open for 6% of the time, Pallas kernels for 0%

commit v1 on v0

--- a/solution.py
+++ b/solution.py
@@ -2,6 +2,15 @@
 import jax.numpy as jnp
 from jax import lax
 from jax.sharding import PartitionSpec as P
+
+
+def plane_test(v0):
+    return jnp.concatenate(
+        jax.lax.all_to_all(
+            jnp.stack(jnp.split(v0, jax.lax.axis_size("batch"), axis=1)), "batch", 0, 0
+        ),
+        axis=0,
+    )
 
 
 def finish_output(attended, gate_logits, norm_gain):
@@ -62,7 +71,7 @@
     )
     attended = attended.reshape(req_dev, length, feature_width)
     local_states = updated.astype(jnp.bfloat16).reshape(req_dev, feature_width, head_size)
-    new_states = lax.all_to_all(local_states, "batch", split_axis=1, concat_axis=0, tiled=True)
+    new_states = plane_test(local_states)
     mixed = finish_output(attended, gate_logits, norm_gain)
     return (mixed, new_states)
 

time: 376 us -> 351 us (0.934)
  local copies, waits for them, and re-layouts: 78.4 us -> 53.9 us
    reshape x1 -> x0, local copies, waits for them, and re-layouts: 35.5 us -> none  [on_device(): updated.astype(jnp.bfloat16).reshape(req_dev, feature_width, head_size)]
    unnamed x24 -> x40, local copies, waits for them, and re-layouts: 20 us -> 35.5 us
    all_to_all x1 -> x0, local copies, waits for them, and re-layouts: 5.21 us -> none  [on_device(): lax.all_to_all(local_states, 'batch', split_axis=1, concat_axis=0, tiled=...]
  transfers between devices with their start and end apart: 3 -> 3, of which waited for: 3 -> 3; matrix products, arithmetic and copies ran while one was open for 6% -> 7% of each run, Pallas kernels for 0% -> 0%
where the time goes in v1:
time: 351 us
  waiting for transfers between devices  165 us (47%)
  local copies, waits for them, and re-layouts  53.9 us (15%)
  other arithmetic  53.9 us (15%)
  blocking collectives  43.8 us (12%)
  starting transfers between devices  17.5 us (5%)
  matrix products  15.4 us (4%)
    all_to_all x1, waiting for transfers between devices, on_device(): lax.all_to_all(chosen, 'batch', split_axis=0, concat_axis=1, tiled=True)  88.3 us
    all_to_all x1, waiting for transfers between devices, plane_test(): jax.lax.all_to_all(jnp.stack(jnp.split(v0, jax.lax.axis_size('batch'), ax...  74.1 us
    unnamed x1, other arithmetic  45.2 us
    unnamed x1, blocking collectives  43.8 us
    unnamed x40, local copies, waits for them, and re-layouts  35.5 us
    dot_general x1, matrix products, attend(): jnp.einsum('rsgd,rsge->rgde', weighted_keys, value_wide, precision=highest)  8.99 us
  transfers between devices with their start and end apart: 3, of which 3 were waited for; matrix products, arithmetic and copies ran while one was open for 7% of the time, Pallas kernels for 0%

profile of v1, /device:TPU:11, one launch (start us, length us, event | category | flops | bytes accessed | tf_op | source)
XLA Modules:
  0.0 350.7 jit_solution(6221129569897583370)
XLA Ops:
  0.6 7.5 %copy.61 = bf16[1,8192,128]{2,0,1:T(2,128)(2,1)} copy(bf16[1,8192,128]{2,1,0:T(8,128)(2,1)} %param.14) | data formatting | bytes 4194304 | tf_op args[6]
  8.1 0.5 broadcast.157
  8.6 45.2 %reduce.1 = bf16[8192,128]{1,0:T(8,128)(2,1)S(1)} reduce(bf16[8192,1,128]{2,1,0:T(2,128)(2,1)} %bitcast.115, bf16[]{:T(256)} %broadcast.157), dimensions={1}, to_apply=%bitcast.95.reduce_sub_computation | reduce | bytes 4194306
  53.8 0.0 copy-start.7
  53.8 0.0 copy-start.6
  53.8 2.0 reshape.205
  55.8 6.5 %all-to-all-start = ((bf16[16,2,32768]{2,1,0:T(2,128)(2,1)}), bf16[16,2,32768]{2,1,0:T(2,128)(2,1)S(1)}, u32[]{:S(2)}, u32[]{:S(2)}) async-start(bf16[16,2,32768]{2,1,0:T(2,128)(2,1)} %reshape.205), calls=%async_computation | async-start | bytes 4194304 | tf_op jit(solution)/shard_map/all_to_all | solution.py:60
  62.3 0.0 copy-done.7
  62.3 0.6 dynamic-slice
  63.6 0.0 copy-done.6
  63.6 0.2 dynamic-update-slice
  63.8 43.8 %all-reduce = s32[32]{0:T(128)S(1)} all-reduce(s32[32]{0:T(128)S(1)} %dynamic-update-slice), channel_id=1, replica_groups=mesh['groups'=2,'batch'=16] {'batch'}, use_global_device_ids=true, to_apply=%add | all-reduce | flops 32 | bytes 256
  107.7 2.2 all-to-all-done
  109.9 6.7 %reshape.206 = bf16[8192,1,128]{2,1,0:T(2,128)(2,1)} reshape(bf16[16,2,32768]{2,1,0:T(2,128)(2,1)S(1)} %all-to-all-done) | data formatting | bytes 4194304
  116.6 2.5 copy.43
  119.1 3.1 gather_fusion
  122.2 4.7 %broadcast_select_fusion = bf16[32,512,128]{2,1,0:T(8,128)(2,1)} fusion(bf16[32,512,128]{2,1,0:T(8,128)(2,1)} %gather_fusion, pred[32]{0:T(512)(128)(4,1)S(1)} %compare_and_fusion), kind=kLoop, calls=%fused_computation.2 | loop fusion | flops 2097152 | bytes 8388640 | tf_op jit(solution)/shard_map/jit(_take)/select_n | solution.py:61
  126.8 0.0 copy-start.2
  126.8 6.2 %all-to-all-start.1 = ((bf16[32,512,128]{2,1,0:T(8,128)(2,1)}), bf16[32,512,128]{2,1,0:T(8,128)(2,1)}, u32[]{:S(2)}, u32[]{:S(2)}) async-start(bf16[32,512,128]{2,1,0:T(8,128)(2,1)} %broadcast_select_fusion), calls=%async_computation.1 | async-start | bytes 8388608 | tf_op jit(solution)/shard_map/all_to_all | solution.py:62
  133.1 0.0 copy-done.2
  133.1 0.0 copy-start.5
  133.1 0.9 reshape.186
  134.0 3.2 reshape.187
  137.2 0.0 copy-done.5
  137.2 0.1 multiply_exponential_fusion
  137.3 88.3 %all-to-all-done.1 = bf16[32,512,128]{2,1,0:T(8,128)(2,1)} async-done(((bf16[32,512,128]{2,1,0:T(8,128)(2,1)}), bf16[32,512,128]{2,1,0:T(8,128)(2,1)}, u32[]{:S(2)}, u32[]{:S(2)}) %all-to-all-start.1) | async-done | bytes 4194336 | tf_op jit(solution)/shard_map/all_to_all | solution.py:62
  225.6 2.6 copy.32
  228.2 0.0 copy-start
  228.2 9.0 %add_convert_fusion = bf16[2,64,128,128]{3,2,1,0:T(8,128)(2,1)S(1)} fusion(bf16[2,64,128,128]{3,2,1,0:T(8,128)(2,1)S(1)} %bitcast.96, f32[64]{0:T(128)S(1)} %multiply_exponential_fusion.2, f32[34,64]{0,1:T(8,128)S(1)} %get-tuple-element.2, bf16[2,34,64,128]{3,2,0,1:T(8,128)(2,1)S(1)} %reshape.187, bf16[2,34,64,128]{3,2,0,1:T(8,128)(2,1)S(1)} %reshape.186), kind=kOutput, calls=%fused_computation.1 | convolution fusion | flops 865140736 | bytes 10625792 | tf_op jit(solution)/shard_map/rsgd,rsge->rgde/dot_general | solution.py:49
  237.2 0.0 copy-done
  237.2 0.7 fusion.28
  238.0 0.7 fusion.27
  238.7 0.7 fusion.26
  239.4 0.7 fusion.25
  240.1 0.7 fusion.24
  240.9 0.7 fusion.23
  241.6 0.7 fusion.22
  242.3 0.7 fusion.21
  243.0 0.7 fusion.20
  243.8 0.7 fusion.19
  244.5 0.7 fusion.18
  245.2 0.7 fusion.17
  245.9 0.7 fusion.16
  246.7 0.7 fusion.15
  247.4 0.7 fusion.14
  248.1 0.8 fusion.13
  248.9 4.8 %all-to-all-start.2 = ((bf16[16,2,512,128]{3,2,1,0:T(8,128)(2,1)}), bf16[16,2,512,128]{3,2,1,0:T(8,128)(2,1)}, u32[]{:S(2)}, u32[]{:S(2)}) async-start(bf16[16,2,512,128]{3,2,1,0:T(8,128)(2,1)} %fusion.13), calls=%async_computation.2 | async-start | bytes 8388608 | tf_op jit(solution)/shard_map/all_to_all | solution.py:9
  253.6 3.2 reshape.185
  256.8 0.1 subtract_compare_fusion
  256.9 0.1 fusion.29
  257.0 0.2 exponential_select_fusion
  257.2 1.6 fusion.9
  258.8 0.0 copy-start.1
  258.8 3.1 fusion
  261.9 0.0 copy-done.1
  261.9 1.8 multiply_reduce_fusion
  263.7 1.8 copy.38
  265.5 2.8 reshape.188
  268.3 0.1 copy.39
  268.4 0.0 copy-done.3
  268.4 0.0 copy-done.4
  268.4 3.5 %fusion.3 = bf16[2,34,8192]{2,0,1:T(2,128)(2,1)} fusion(bf16[2,34,8192]{2,0,1:T(2,128)(2,1)S(1)} %copy-done.3, f32[2,34,8192]{2,0,1:T(2,128)S(1)} %reshape.188, f32[8192]{0:T(1024)S(1)} %copy-done.4, f32[2,34]{0,1:T(8,128)S(1)} %copy.39), kind=kLoop, calls=%fused_computation.11 | loop fusion | flops 4456448 | bytes 4489488 | tf_op jit(solution)/shard_map/convert_element_type | solution.py:19
  271.9 74.1 %all-to-all-done.2 = bf16[16,2,512,128]{3,2,1,0:T(8,128)(2,1)} async-done(((bf16[16,2,512,128]{3,2,1,0:T(8,128)(2,1)}), bf16[16,2,512,128]{3,2,1,0:T(8,128)(2,1)}, u32[]{:S(2)}, u32[]{:S(2)}) %all-to-all-start.2) | async-done | bytes 4194336 | tf_op jit(solution)/shard_map/all_to_all | solution.py:9
  346.1 4.7 %copy.79 = bf16[32,512,128]{2,1,0:T(8,128)(2,1)} copy(bf16[32,512,128]{2,1,0:T(8,128)(2,1)} %bitcast.24) | data formatting | bytes 8388608
  (10 shorter events, 0.1 us)
Async XLA Ops:
  53.8 8.6 %copy-start.7 = (u32[32]{0:T(128)S(1)}, u32[32]{0:T(128)}, u32[]{:S(2)}) copy-start(u32[32]{0:T(128)} %constant.40) | copy-start | bytes 388
  53.8 9.8 %copy-start.6 = (s32[2]{0:T(128)S(1)}, s32[2]{0:T(128)}, u32[]{:S(2)}) copy-start(s32[2]{0:T(128)} %param.15) | copy-start | bytes 28
  55.8 54.1 %all-to-all-start = ((bf16[16,2,32768]{2,1,0:T(2,128)(2,1)}), bf16[16,2,32768]{2,1,0:T(2,128)(2,1)S(1)}, u32[]{:S(2)}, u32[]{:S(2)}) async-start(bf16[16,2,32768]{2,1,0:T(2,128)(2,1)} %reshape.205), calls=%async_computation | async-start | bytes 4194304 | tf_op jit(solution)/shard_map/all_to_all | solution.py:60
  126.8 6.3 %copy-start.2 = (bf16[2,34,8192]{2,0,1:T(2,128)(2,1)S(1)}, bf16[2,34,8192]{2,0,1:T(2,128)(2,1)}, u32[]{:S(2)}) copy-start(bf16[2,34,8192]{2,0,1:T(2,128)(2,1)} %param.9) | copy-start | bytes 3342340
  126.8 98.7 %all-to-all-start.1 = ((bf16[32,512,128]{2,1,0:T(8,128)(2,1)}), bf16[32,512,128]{2,1,0:T(8,128)(2,1)}, u32[]{:S(2)}, u32[]{:S(2)}) async-start(bf16[32,512,128]{2,1,0:T(8,128)(2,1)} %broadcast_select_fusion), calls=%async_computation.1 | async-start | bytes 8388608 | tf_op jit(solution)/shard_map/all_to_all | solution.py:62
  133.1 4.1 %copy-start.5 = (f32[64]{0:T(128)S(1)}, f32[64]{0:T(128)}, u32[]{:S(2)}) copy-start(f32[64]{0:T(128)} %param.12) | copy-start | bytes 772
  228.2 9.0 %copy-start = (bf16[2,16,512,128]{3,2,1,0:T(8,128)(2,1)}, bf16[2,16,512,128]{3,2,1,0:T(8,128)(2,1)S(1)}, u32[]{:S(2)}) copy-start(bf16[2,16,512,128]{3,2,1,0:T(8,128)(2,1)S(1)} %copy.32) | copy-start | bytes 12582916
  248.9 97.2 %all-to-all-start.2 = ((bf16[16,2,512,128]{3,2,1,0:T(8,128)(2,1)}), bf16[16,2,512,128]{3,2,1,0:T(8,128)(2,1)}, u32[]{:S(2)}, u32[]{:S(2)}) async-start(bf16[16,2,512,128]{3,2,1,0:T(8,128)(2,1)} %fusion.13), calls=%async_computation.2 | async-start | bytes 8388608 | tf_op jit(solution)/shard_map/all_to_all | solution.py:9
  258.8 3.1 copy-start.1
  263.7 4.7 %copy-start.3 = (bf16[2,34,8192]{2,0,1:T(2,128)(2,1)S(1)}, bf16[2,34,8192]{2,0,1:T(2,128)(2,1)}, u32[]{:S(2)}) copy-start(bf16[2,34,8192]{2,0,1:T(2,128)(2,1)} %param.11) | copy-start | bytes 3342340
  263.7 4.7 %copy-start.4 = (f32[8192]{0:T(1024)S(1)}, f32[8192]{0:T(1024)}, u32[]{:S(2)}) copy-start(f32[8192]{0:T(1024)} %param.13) | copy-start | bytes 98308
